TPU v7x, 1024 devices: a whole 8x8x8 slice. The times are simulated.
1024 devices in a mesh: chan: 64 (over z_lo, x, core), tile: 16 (over y, z_hi).
Axes of the slice: x: 8, y: 8, z: 8 (z_hi: 2, z_lo: 4; z = z_hi * 4 + z_lo), core: 2. Of those that a mesh axis runs over, the one named last changes fastest.
Arguments:
- voltages: bfloat16 [16, 128, 555008], P('tile', 'chan'), may hold values from -6 to 6
- fir_taps: float32 [16, 2048], replicated, may hold values from -4 to 4
- channels: int32 [64], replicated, may hold values from 0 to 2047
- input_good_mask: int32 [16, 128], P('tile', 'chan'), may hold values 0 or 1
- tile_map: int32 [64, 16], replicated, may hold values from 0 to 15, each once within a row
Outputs:
- visibilities: bfloat16 [64, 16, 2, 512, 512], P('chan', 'tile')
Inputs may be any that keep to these rules, and one draw needn't show every extreme that they name: `tile_map`: for every channel, every tile of the 4 x 4 grid, numbered row by row, stands in exactly one slot.
All inputs are finite; a program needn't handle non-finite values. No bound on the sum of `input_good_mask` on one device may be relied on, other than what follows from the above.
Results may differ from a plain program's by a relative error of at most 0.0077.
Values may be sent and summed in bfloat16 or wider, within the bound.
A program may use at most 32 MiB of HBM per device.

v0:
```python
import math

import jax
import jax.numpy as jnp
from jax import lax
from jax.sharding import PartitionSpec as P

TRANSFORM_LENGTH = 2048
FILTER_TAPS = 16
SPECTRA_SUMMED = 256


def dft_rows(channels):
    sample = jnp.arange(TRANSFORM_LENGTH, dtype=jnp.int32)
    phase = channels[:, None] * sample[None, :] % TRANSFORM_LENGTH
    angle = phase.astype(jnp.float32) * (2.0 * math.pi / TRANSFORM_LENGTH)
    factor = 1.0 / math.sqrt(TRANSFORM_LENGTH)
    return jnp.concatenate([jnp.cos(angle) * factor, -jnp.sin(angle) * factor], axis=0).astype(
        jnp.bfloat16
    )


def on_device(voltages, fir_taps, channels, input_good_mask, tile_map):
    antennas_per_device = voltages.shape[1]
    sample_block = voltages.reshape(
        antennas_per_device, SPECTRA_SUMMED + FILTER_TAPS - 1, TRANSFORM_LENGTH
    )
    running_total = jnp.zeros((antennas_per_device, SPECTRA_SUMMED, TRANSFORM_LENGTH), jnp.float32)
    for tap_index in range(FILTER_TAPS):
        running_total = running_total + fir_taps[tap_index][None, None, :] * sample_block[
            :, tap_index : tap_index + SPECTRA_SUMMED, :
        ].astype(jnp.float32)
    filtered = running_total.astype(jnp.bfloat16)
    dft_table = dft_rows(channels)
    device_spectra = jnp.einsum(
        "kn,asn->kas", dft_table, filtered, preferred_element_type=jnp.float32
    )
    column_flags = input_good_mask.reshape(1, antennas_per_device, 1).astype(jnp.float32)
    device_spectra = (device_spectra * column_flags).astype(jnp.bfloat16)
    device_spectra = device_spectra.reshape(
        2, channels.shape[0], antennas_per_device, SPECTRA_SUMMED
    )
    turned = lax.all_to_all(device_spectra, "chan", split_axis=1, concat_axis=2, tiled=True)
    tiles_axis = lax.axis_size("tile")
    grid_side = tiles_axis // 8 + 2
    inputs_all = turned.shape[2] * tiles_axis
    side = inputs_all // grid_side
    slot_tiles = lax.dynamic_index_in_dim(
        tile_map, lax.axis_index("chan") * turned.shape[1], 0, keepdims=False
    )
    tile = lax.dynamic_index_in_dim(slot_tiles, lax.axis_index("tile"), 0, keepdims=False)
    row_start = tile // grid_side * side
    col_start = tile % grid_side * side
    whole = lax.all_gather(turned, "tile", axis=2, tiled=True)
    rows = lax.dynamic_slice_in_dim(whole, row_start, side, 2)
    cols = lax.dynamic_slice_in_dim(whole, col_start, side, 2)
    swapped = jnp.stack([cols[1], -cols[0]], axis=0)
    real_part = jnp.einsum("xcis,xcjs->cij", rows, cols, preferred_element_type=jnp.float32)
    imag_part = jnp.einsum("xcis,xcjs->cij", rows, swapped, preferred_element_type=jnp.float32)
    visible = (jnp.stack([real_part, imag_part], axis=1) * (1.0 / SPECTRA_SUMMED)).astype(
        jnp.bfloat16
    )
    return visible.reshape(visible.shape[0], 1, 2, side, side)


def solution(mesh):
    in_specs = (P("tile", "chan", None), P(), P(), P("tile", "chan"), P())
    out_specs = P("chan", "tile", None, None, None)
    return jax.shard_map(
        on_device, mesh=mesh, in_specs=in_specs, out_specs=out_specs, check_vma=False
    )
```

profile of v0, /device:TPU:2, one launch (start us, length us, event | category | flops | bytes accessed | tf_op | source)
XLA Modules:
  0.0 178.2 jit_solution(11402101647406654056)
XLA Ops:
  6.5 0.0 all-gather.2.cloned.1.call-start
  6.5 0.7 convert_bitcast_fusion
  7.2 1.9 %fusion.24 = (f32[1,2048]{1,0:T(1,128)S(1)}, f32[1,2048]{1,0:T(1,128)S(1)}, f32[1,2048]{1,0:T(1,128)S(1)}, f32[1,2048]{1,0:T(1,128)S(1)}, f32[1,2048]{1,0:T(1,12...) fusion(f32[16,2048]{1,0:T(8,128)} %param.6), kind=kLoop, calls=%fused_computation.38 | loop fusion | bytes 262144 | tf_op jit(solution)/shard_map/slice | solution.py:30
  9.1 3.1 %multiply_convert_fusion.1 = (bf16[64,2048]{1,0:T(8,128)(2,1)S(1)}, bf16[64,2048]{1,0:T(8,128)(2,1)S(1)}) fusion(s32[64]{0:T(128)} %param.7), kind=kLoop, calls=%fused_computation.25 | loop fusion | flops 2490368 | bytes 524544 | tf_op jit(solution)/shard_map/convert
  12.3 3.0 %reshape.99 = bf16[2,271,2048]{2,1,0:T(8,128)(2,1)S(1)} reshape(bf16[1,2,555008]{2,1,0:T(2,128)(2,1)} %param.5) | data formatting | bytes 4440064 | tf_op jit(solution)/shard_map/reshape | solution.py:25
  15.3 8.3 %fusion.3 = bf16[128,2,256]{2,0,1:T(8,128)(2,1)S(1)} fusion(bf16[2,271,2048]{2,1,0:T(8,128)(2,1)S(1)} %reshape.99, f32[2048]{0:T(1024)S(1)} %bitcast.59, f32[2048]{0:T(1024)S(1)} %bitcast.60, f32[2048]{0:T(1024)S(1)} %bitcast.46, f32[2048]{0:T(1024)S(1)} %bitcast.47, f32[2048]{0:T(1024)S(1)} %bitcast.48, f32[2048]{0:T(1024)S(1)} %bitcast.49, ...), kind=kOutput, calls=%fused_computation.7 | convolution fusion | flops 319946752 | bytes 34341376 | tf_op jit(solution)/shard_map/kn,asn->kas/dot_general | solution.py:35
  23.6 0.1 copy.8
  23.7 26.2 %all_to_all.12 = bf16[2,64,2,256]{3,0,2,1:T(2,128)(2,1)S(1)} all-to-all(bf16[2,64,2,256]{3,0,2,1:T(2,128)(2,1)S(1)} %copy.8), channel_id=1, replica_groups=mesh['chan'=64,'tile'=16] {'chan'}, dimensions={1} | all-to-all | bytes 262144 | tf_op jit(solution)/shard_map/all_to_all | solution.py:43
  50.0 0.7 copy.10
  50.6 0.0 all-gather.2.cloned.1.call-update
  50.7 1.3 dynamic_slice.12
  54.2 111.6 %all-gather.2.cloned.1.call-done = bf16[2,1,2048,256]{3,2,0,1:T(8,128)(2,1)} async-done(((bf16[2,1,128,256]{3,2,0,1:T(8,128)(2,1)}), bf16[2,1,2048,256]{3,2,0,1:T(8,128)(2,1)}) %all-gather.2.cloned.1.call-update) | async-done | bytes 2097168 | tf_op jit(solution)/shard_map/all_gather | solution.py:54
  165.8 1.1 constant_dynamic-slice_fusion
  166.9 1.7 convolution_bitcast_fusion.1
  168.6 1.5 convolution_bitcast_fusion
  170.1 1.3 fusion
Async XLA Ops:
  6.5 159.3 %all-gather.2.cloned.1.call-start = ((), (), s32[]{:S(2)}) async-start(), calls=%async_computation.1 | async-start | bytes 2228224 | tf_op jit(solution)/shard_map/all_gather | solution.py:54
Sparse Core Ops, SparseCore 0:
  50.8 115.0 all-gather.1
where the time goes:
time: 179 us; the launch traced here: 178 us
  waiting for transfers between devices  112 us (63%)
  blocking collectives  26.2 us (15%)
  between operations  15.7 us (9%)
  matrix products  11.5 us (6%)
  local copies, waits for them, and re-layouts  6.99 us (4%)
  other arithmetic  6.14 us (3%)
    all_gather x1, waiting for transfers between devices, on_device(): whole = lax.all_gather(turned, 'tile', axis=2, tiled=True)  112 us
    all_to_all x1, blocking collectives, on_device(): lax.all_to_all(device_spectra, 'chan', split_axis=1, concat_axis=2, tiled...  26.2 us
    dot_general x1, matrix products, on_device(): jnp.einsum('kn,asn->kas', dft_table, filtered, preferred_element_type=jnp...  8.3 us
  transfers between devices with their start and end apart: 1, of which 1 were waited for; matrix products, arithmetic and copies ran while one was open for 1% of the time, Pallas kernels for 0%

commit v1 on v0

v1 whole, which is shorter than its diff:
```python
import math

import jax
import jax.numpy as jnp
from jax import lax
from jax.experimental import pallas as pl
from jax.experimental.pallas import tpu as pltpu
from jax.sharding import PartitionSpec as P

TRANSFORM_LENGTH = 2048
FILTER_TAPS = 16
SPECTRA_SUMMED = 256
MESH = pl.DeviceIdType.MESH


def dft_rows(channels):
    sample = jnp.arange(TRANSFORM_LENGTH, dtype=jnp.int32)
    phase = channels[:, None] * sample[None, :] % TRANSFORM_LENGTH
    angle = phase.astype(jnp.float32) * (2.0 * math.pi / TRANSFORM_LENGTH)
    factor = 1.0 / math.sqrt(TRANSFORM_LENGTH)
    return jnp.concatenate([jnp.cos(angle) * factor, -jnp.sin(angle) * factor], axis=0).astype(
        jnp.bfloat16
    )


def correlate_kernel(
    n_chan, n_tile, map_ref, send_ref, out_ref, turned, whole,
    turn_send, turn_recv, ring_send, ring_recv, pair_send, pair_recv,
):
    me = lax.axis_index("chan")
    here = lax.axis_index("tile")
    ahead, behind = lax.rem(here + 2, n_tile), lax.rem(here + n_tile - 2, n_tile)
    pair = here + 1 - 2 * lax.rem(here, 2)
    block_rows, width = whole.shape[1], whole.shape[2]
    grid_side = n_tile // 8 + 2
    side = block_rows * n_tile // grid_side

    barrier = pltpu.get_barrier_semaphore()

    def greet(step, _):
        peer = lax.rem(me + step, n_chan)
        pl.semaphore_signal(barrier, inc=1, device_id={"chan": peer}, device_id_type=MESH)
        return 0

    lax.fori_loop(1, n_chan, greet, 0)
    for other in (ahead, behind, pair):
        pl.semaphore_signal(barrier, inc=1, device_id={"tile": other}, device_id_type=MESH)
    pl.semaphore_wait(barrier, n_chan - 1 + 3)

    def turn(step, _):
        peer = lax.rem(me + step, n_chan)
        pltpu.make_async_remote_copy(
            src_ref=send_ref.at[peer], dst_ref=turned.at[me], send_sem=turn_send,
            recv_sem=turn_recv, device_id={"chan": peer}, device_id_type=MESH,
        ).start()
        return 0

    lax.fori_loop(1, n_chan, turn, 0)
    turned[me] = send_ref[me]
    pltpu.make_async_remote_copy(
        src_ref=send_ref.at[pl.ds(0, n_chan - 1)], dst_ref=turned.at[pl.ds(0, n_chan - 1)],
        send_sem=turn_send, recv_sem=turn_recv, device_id={"chan": me}, device_id_type=MESH,
    ).wait()
    whole[here] = turned[...].reshape(block_rows, width)

    def hop(direction, column, step):
        base = here if column == 0 else pair
        back = -2 * (step - 1) if direction == 0 else 2 * (step - 1)
        block = lax.rem(base + n_tile + back, n_tile)
        piece = whole.at[block]
        if step == n_tile // 4:
            half = block_rows // 2
            piece = whole.at[block, pl.ds(direction * half, half)]
        index = (direction, column, step - 1)
        return pltpu.make_async_remote_copy(
            src_ref=piece, dst_ref=piece, send_sem=ring_send.at[index],
            recv_sem=ring_recv.at[index],
            device_id={"tile": ahead if direction == 0 else behind}, device_id_type=MESH,
        )

    across = pltpu.make_async_remote_copy(
        src_ref=whole.at[here], dst_ref=whole.at[here], send_sem=pair_send, recv_sem=pair_recv,
        device_id={"tile": pair}, device_id_type=MESH,
    )
    across.start()
    last = n_tile // 4
    order = [(0, 1), (0, 2), (1, 1), (0, 3), (1, 2), (0, 4), (1, 3), (1, 4)]
    for column, step in order:
        if step == 1 and column == 1:
            across.wait_recv()
        for direction in (0, 1):
            if step > 1:
                hop(direction, column, step - 1).wait_recv()
            hop(direction, column, step).start()
    for column in (0, 1):
        for direction in (0, 1):
            hop(direction, column, last).wait_recv()
    across.wait_send()
    for column, step in order:
        for direction in (0, 1):
            hop(direction, column, step).wait_send()

    tile = map_ref[me, here]
    per_side = n_tile // grid_side
    rows = whole[pl.ds(lax.div(tile, grid_side) * per_side, per_side)].reshape(side, width)
    cols = whole[pl.ds(lax.rem(tile, grid_side) * per_side, per_side)].reshape(side, width)
    half = width // 2
    swapped = jnp.concatenate([cols[:, half:], -cols[:, :half]], axis=1)
    contract = (((1,), (1,)), ((), ()))
    scale = 1.0 / SPECTRA_SUMMED
    real_part = lax.dot_general(rows, cols, contract, preferred_element_type=jnp.float32)
    out_ref[0, 0, 0] = (real_part * scale).astype(out_ref.dtype)
    imag_part = lax.dot_general(rows, swapped, contract, preferred_element_type=jnp.float32)
    out_ref[0, 0, 1] = (imag_part * scale).astype(out_ref.dtype)


def on_device(voltages, fir_taps, channels, input_good_mask, tile_map):
    antennas = voltages.shape[1]
    sample_block = voltages.reshape(antennas, SPECTRA_SUMMED + FILTER_TAPS - 1, TRANSFORM_LENGTH)
    running_total = jnp.zeros((antennas, SPECTRA_SUMMED, TRANSFORM_LENGTH), jnp.float32)
    for tap_index in range(FILTER_TAPS):
        running_total = running_total + fir_taps[tap_index][None, None, :] * sample_block[
            :, tap_index : tap_index + SPECTRA_SUMMED, :
        ].astype(jnp.float32)
    filtered = running_total.astype(jnp.bfloat16)
    dft_table = dft_rows(channels)
    spectra = jnp.einsum("kn,asn->kas", dft_table, filtered, preferred_element_type=jnp.float32)
    flags = input_good_mask.reshape(1, antennas, 1).astype(jnp.float32)
    spectra = (spectra * flags).astype(jnp.bfloat16)
    n_channels = channels.shape[0]
    n_chan, n_tile = lax.axis_size("chan"), lax.axis_size("tile")
    spectra = spectra.reshape(2, n_channels, antennas, SPECTRA_SUMMED)
    send = jnp.transpose(spectra, (1, 2, 0, 3)).reshape(n_channels, antennas, 2 * SPECTRA_SUMMED)

    block_rows, width = antennas * n_chan, 2 * SPECTRA_SUMMED
    side = block_rows * n_tile // (n_tile // 8 + 2)
    vmem = pl.BlockSpec(memory_space=pltpu.VMEM)
    hops = (2, 2, n_tile // 4)
    return pl.pallas_call(
        lambda *refs: correlate_kernel(n_chan, n_tile, *refs),
        name="correlate",
        out_shape=jax.ShapeDtypeStruct((1, 1, 2, side, side), jnp.bfloat16),
        in_specs=[pl.BlockSpec(memory_space=pltpu.SMEM), vmem],
        out_specs=vmem,
        scratch_shapes=[
            pltpu.VMEM((n_chan, antennas, width), jnp.bfloat16),
            pltpu.VMEM((n_tile, block_rows, width), jnp.bfloat16),
            pltpu.SemaphoreType.DMA,
            pltpu.SemaphoreType.DMA,
            pltpu.SemaphoreType.DMA(hops),
            pltpu.SemaphoreType.DMA(hops),
            pltpu.SemaphoreType.DMA,
            pltpu.SemaphoreType.DMA,
        ],
        compiler_params=pltpu.CompilerParams(
            collective_id=0, has_side_effects=True, vmem_limit_bytes=32 * 1024 * 1024
        ),
    )(tile_map, send)


def solution(mesh):
    in_specs = (P("tile", "chan", None), P(), P(), P("tile", "chan"), P())
    out_specs = P("chan", "tile", None, None, None)
    return jax.shard_map(
        on_device, mesh=mesh, in_specs=in_specs, out_specs=out_specs, check_vma=False
    )
```

time: 179 us -> 76 us (0.42)
  the two profiles are of different devices: /device:TPU:2 before, /device:TPU:32 now
where the time goes in v1:
time: 76 us; the launch traced here: 75.7 us
  Pallas kernels  58 us (76%)
  matrix products  8.3 us (11%)
  local copies, waits for them, and re-layouts  6.19 us (8%)
  other arithmetic  3.15 us (4%)
    pallas_call x1, Pallas kernels, on_device(): pl.pallas_call(lambda *refs: correlate_kernel(n_chan, n_tile, *refs), nam...  58 us
    dot_general x1, matrix products, on_device(): jnp.einsum('kn,asn->kas', dft_table, filtered, preferred_element_type=jnp...  8.3 us
    another operation x1, other arithmetic  3.15 us
    reshape x1, local copies, waits for them, and re-layouts, on_device(): voltages.reshape(antennas, SPECTRA_SUMMED + FILTER_TAPS - 1, TRANSFORM_LE...  2.98 us
    slice x1, local copies, waits for them, and re-layouts, on_device(): fir_taps[tap_index][None, None, :]  1.92 us

profile of v1, /device:TPU:32, one launch (start us, length us, event | category | flops | bytes accessed | tf_op | source)
XLA Modules:
  0.0 75.7 jit_solution(17579551378194183346)
XLA Ops:
  0.0 1.9 %fusion.12 = (f32[1,2048]{1,0:T(1,128)S(1)}, f32[1,2048]{1,0:T(1,128)S(1)}, f32[1,2048]{1,0:T(1,128)S(1)}, f32[1,2048]{1,0:T(1,128)S(1)}, f32[1,2048]{1,0:T(1,12...) fusion(f32[16,2048]{1,0:T(8,128)} %param.6), kind=kLoop, calls=%fused_computation.21 | loop fusion | bytes 262144 | tf_op jit(solution)/shard_map/slice | solution.py:122
  1.9 3.1 %multiply_convert_fusion.1 = (bf16[64,2048]{1,0:T(8,128)(2,1)S(1)}, bf16[64,2048]{1,0:T(8,128)(2,1)S(1)}) fusion(s32[64]{0:T(128)} %param.7), kind=kLoop, calls=%fused_computation.14 | loop fusion | flops 2490368 | bytes 524544 | tf_op jit(solution)/shard_map/convert
  5.1 0.0 copy-start.1
  5.1 3.0 %reshape.35 = bf16[2,271,2048]{2,1,0:T(8,128)(2,1)S(1)} reshape(bf16[1,2,555008]{2,1,0:T(2,128)(2,1)} %param.5) | data formatting | bytes 4440064 | tf_op jit(solution)/shard_map/reshape | solution.py:119
  8.1 0.0 copy-done.1
  8.1 0.0 copy-start
  8.1 8.3 %fusion.2 = bf16[128,2,256]{2,0,1:T(8,128)(2,1)S(1)} fusion(bf16[2,271,2048]{2,1,0:T(8,128)(2,1)S(1)} %reshape.35, f32[2048]{0:T(1024)S(1)} %bitcast.41, f32[2048]{0:T(1024)S(1)} %bitcast.42, f32[2048]{0:T(1024)S(1)} %bitcast.28, f32[2048]{0:T(1024)S(1)} %bitcast.29, f32[2048]{0:T(1024)S(1)} %bitcast.30, f32[2048]{0:T(1024)S(1)} %bitcast.31, ...), kind=kOutput, calls=%fused_computation.3 | convolution fusion | flops 319946752 | bytes 34341376 | tf_op jit(solution)/shard_map/kn,asn->kas/dot_general | solution.py:127
  16.4 0.1 copy.11
  16.6 0.1 reshape.37.refs_1_
  16.7 0.0 copy-done
  16.7 0.1 copy.9.refs_0_
  16.7 58.0 %correlate.1 = bf16[1,1,2,512,512]{4,3,2,1,0:T(8,128)(2,1)S(1)} custom-call(s32[64,16]{1,0:T(8,128)S(1)} %copy.9.refs_0_, bf16[64,2,512]{2,1,0:T(2,128)(2,1)S(1)} %reshape.37.refs_1_), custom_call_target="tpu_custom_call" | custom-call | tf_op jit(solution)/shard_map/correlate/pallas_call | solution.py:139
  74.7 1.0 %copy.13 = bf16[1,1,2,512,512]{4,3,2,1,0:T(8,128)(2,1)} copy(bf16[1,1,2,512,512]{4,3,2,1,0:T(8,128)(2,1)S(1)} %correlate.1) | data formatting | bytes 2097152
  (1 shorter events, 0.0 us)
Async XLA Ops:
  5.1 3.0 %copy-start.1 = (s32[1,2]{1,0:T(1,128)S(1)}, s32[1,2]{1,0:T(1,128)}, u32[]{:S(2)}) copy-start(s32[1,2]{1,0:T(1,128)} %param.8) | copy-start | bytes 28
  8.1 8.6 %copy-start = (s32[64,16]{0,1:T(8,128)S(1)}, s32[64,16]{0,1:T(8,128)}, u32[]{:S(2)}) copy-start(s32[64,16]{0,1:T(8,128)} %param.9) | copy-start | bytes 12292

commit v2 on v0

v2 whole, which is shorter than its diff:
```python
import math

import jax
import jax.numpy as jnp
from jax import lax
from jax.experimental import pallas as pl
from jax.experimental.pallas import tpu as pltpu
from jax.sharding import PartitionSpec as P

TRANSFORM_LENGTH = 2048
FILTER_TAPS = 16
SPECTRA_SUMMED = 256
MESH = pl.DeviceIdType.MESH

LANES = 128
GROUPS = TRANSFORM_LENGTH // LANES
FRAMES = SPECTRA_SUMMED + FILTER_TAPS - 1
CHUNK = LANES
CHUNKS = SPECTRA_SUMMED // CHUNK
BY_LANES = (((1,), (1,)), ((), ()))

RING_ORDER = (
    (0, 0, 1), (1, 0, 1), (0, 0, 2), (1, 0, 2), (0, 1, 1), (0, 0, 3), (1, 0, 3), (1, 1, 1),
    (0, 1, 2), (0, 0, 4), (1, 0, 4), (1, 1, 2), (0, 1, 3), (1, 1, 3), (0, 1, 4), (1, 1, 4),
)


def fill_table(channels_row, table):
    n = channels_row.shape[1]
    down = lax.broadcasted_iota(jnp.int32, (n, n), 0)
    along = lax.broadcasted_iota(jnp.int32, (n, n), 1)
    picked = jnp.where(down == along, channels_row.astype(jnp.float32), 0.0)
    lane = lax.broadcasted_iota(jnp.int32, (n, LANES), 1).astype(jnp.float32)
    phase = jnp.sum(picked, axis=1, keepdims=True) * lane
    low = phase - TRANSFORM_LENGTH * jnp.floor(phase * (1.0 / TRANSFORM_LENGTH))
    low = low * (2.0 * math.pi / TRANSFORM_LENGTH)
    high = phase - GROUPS * jnp.floor(phase * (1.0 / GROUPS))
    high = high * (2.0 * math.pi / GROUPS)
    factor = 1.0 / math.sqrt(TRANSFORM_LENGTH)
    cos_low, sin_low = jnp.cos(low) * factor, jnp.sin(low) * factor
    cos_high, sin_high = jnp.cos(high), jnp.sin(high)
    for group in range(GROUPS):
        lanes = pl.ds(group * LANES, LANES)
        cos_g, sin_g = cos_high[:, group : group + 1], sin_high[:, group : group + 1]
        table[pl.ds(0, n), lanes] = (cos_g * cos_low - sin_g * sin_low).astype(table.dtype)
        table[pl.ds(n, n), lanes] = (-(sin_g * cos_low + cos_g * sin_low)).astype(table.dtype)


def filter_group(group, chunk, slab, wide, taps, filtered):
    rows = 2 * (CHUNK + FILTER_TAPS)
    samples = slab.at[group].reshape(slab.shape[1] * 2, LANES)
    for row in range(0, rows, 16):
        wide[pl.ds(row, 16), :] = samples[pl.ds(2 * CHUNK * chunk + row, 16), :].astype(jnp.float32)
    lanes = pl.ds(group * LANES, LANES)
    weight = [jnp.broadcast_to(taps[pl.ds(j, 1), lanes], (8, LANES)) for j in range(FILTER_TAPS)]
    for antenna in (0, 1):
        for base in range(0, CHUNK, 64):
            total = [None] * 8
            for frame in range(64 + FILTER_TAPS - 8):
                window = wide[pl.ds(2 * (base + frame) + antenna, 8, stride=2), :]
                for part in range(8):
                    j = frame - 8 * part
                    if 0 <= j < FILTER_TAPS:
                        term = weight[j] * window
                        total[part] = term if total[part] is None else total[part] + term
            for part in range(0, 8, 2):
                pair = jnp.concatenate([total[part], total[part + 1]], axis=0)
                place = pl.ds(antenna * CHUNK + base + 8 * part, 16)
                filtered[place, lanes] = pair.astype(filtered.dtype)


def kernel(
    n_chan, n_tile, volts, taps_hbm, channels, flags, tile_map, out,
    slab, taps, wide, filtered, table, mixed, gathered, totals, *rest,
):
    send, whole = rest[:CHUNKS], rest[CHUNKS : 2 * CHUNKS]
    load_sem, taps_sem, turn_send, turn_recv, ring_send, ring_recv, pair_send, pair_recv = rest[
        2 * CHUNKS :
    ]
    me = lax.axis_index("chan")
    here = lax.axis_index("tile")
    ahead, behind = lax.rem(here + 2, n_tile), lax.rem(here + n_tile - 2, n_tile)
    pair = here + 1 - 2 * lax.rem(here, 2)
    last = n_tile // 4
    grid_side = n_tile // 8 + 2
    side = 2 * n_chan * n_tile // grid_side

    def load(group):
        return pltpu.make_async_copy(
            volts.at[:, group], slab.at[group, pl.ds(0, FRAMES)], load_sem.at[group]
        )

    load_taps = pltpu.make_async_copy(taps_hbm, taps, taps_sem)
    load_taps.start()
    for group in range(GROUPS):
        load(group).start()

    barrier = pltpu.get_barrier_semaphore()

    def greet(step, _):
        peer = lax.rem(me + step, n_chan)
        pl.semaphore_signal(barrier, inc=1, device_id={"chan": peer}, device_id_type=MESH)
        return 0

    lax.fori_loop(1, n_chan, greet, 0)
    for other in (ahead, behind, pair):
        pl.semaphore_signal(barrier, inc=1, device_id={"tile": other}, device_id_type=MESH)

    fill_table(channels[...], table)
    load_taps.wait()

    for chunk in range(CHUNKS):

        def filter_step(group, _):
            if chunk == 0:
                load(group).wait()
            filter_group(group, chunk, slab, wide, taps, filtered)
            return 0

        lax.fori_loop(0, GROUPS, filter_step, 0)
        spectra = lax.dot_general(
            table[...], filtered[...], BY_LANES, preferred_element_type=jnp.float32
        )
        for part in (0, 1):
            for antenna in (0, 1):
                flag = flags[0, antenna].astype(jnp.float32)
                block = spectra[
                    part * n_chan : (part + 1) * n_chan, antenna * CHUNK : (antenna + 1) * CHUNK
                ]
                mixed[pl.ds(antenna, n_chan, stride=2), :] = block * flag
            packed = send[chunk].at[part].reshape(2 * n_chan, LANES)
            packed[...] = mixed[...].astype(packed.dtype)
        if chunk == 0:
            pl.semaphore_wait(barrier, n_chan - 1 + 3)

        def turn(step, _):
            peer = lax.rem(me + step, n_chan)
            pltpu.make_async_remote_copy(
                src_ref=send[chunk].at[:, peer], dst_ref=whole[chunk].at[:, here, me],
                send_sem=turn_send.at[chunk], recv_sem=turn_recv.at[chunk],
                device_id={"chan": peer}, device_id_type=MESH,
            ).start()
            return 0

        lax.fori_loop(1, n_chan, turn, 0)
        whole[chunk][:, here, me] = send[chunk][:, me]

    def turned(chunk):
        return pltpu.make_async_remote_copy(
            src_ref=send[chunk].at[:, pl.ds(0, n_chan - 1)],
            dst_ref=whole[chunk].at[:, here, pl.ds(0, n_chan - 1)],
            send_sem=turn_send.at[chunk], recv_sem=turn_recv.at[chunk],
            device_id={"chan": me}, device_id_type=MESH,
        )

    def across(chunk):
        block = whole[chunk].at[:, here]
        return pltpu.make_async_remote_copy(
            src_ref=block, dst_ref=block, send_sem=pair_send.at[chunk],
            recv_sem=pair_recv.at[chunk], device_id={"tile": pair}, device_id_type=MESH,
        )

    def hop(chunk, direction, column, step):
        base = here if column == 0 else pair
        back = -2 * (step - 1) if direction == 0 else 2 * (step - 1)
        block = lax.rem(base + n_tile + back, n_tile)
        piece = whole[chunk].at[direction, block] if step == last else whole[chunk].at[:, block]
        index = (chunk, direction, column, step - 1)
        return pltpu.make_async_remote_copy(
            src_ref=piece, dst_ref=piece, send_sem=ring_send.at[index],
            recv_sem=ring_recv.at[index],
            device_id={"tile": ahead if direction == 0 else behind}, device_id_type=MESH,
        )

    for chunk, column, step in RING_ORDER:
        if step == 1 and column == 0:
            turned(chunk).wait()
            across(chunk).start()
        if step == 1 and column == 1:
            across(chunk).wait_recv()
        for direction in (0, 1):
            if step > 1:
                hop(chunk, direction, column, step - 1).wait_recv()
            hop(chunk, direction, column, step).start()

    tile = tile_map[here, me]
    for chunk in range(CHUNKS):
        for column in (0, 1):
            for direction in (0, 1):
                hop(chunk, direction, column, last).wait_recv()
        across(chunk).wait_send()
        for _, column, step in [entry for entry in RING_ORDER if entry[0] == chunk]:
            for direction in (0, 1):
                hop(chunk, direction, column, step).wait_send()
        inputs = 2 * n_chan * n_tile
        flat = whole[chunk].reshape(2 * inputs, LANES)
        for part in (0, 1):
            for block in range(grid_side):
                gathered[block, :, part * LANES : (part + 1) * LANES] = flat[
                    pl.ds(part * inputs + block * side, side), :
                ]
        rows = gathered[lax.div(tile, grid_side)]
        straight = gathered[lax.rem(tile, grid_side)]
        crossed = jnp.concatenate([straight[:, LANES:], -straight[:, :LANES]], axis=1)
        for part, cols in enumerate((straight, crossed)):
            product = lax.dot_general(rows, cols, BY_LANES, preferred_element_type=jnp.float32)
            if chunk > 0:
                product = product + totals[part]
            if chunk < CHUNKS - 1:
                totals[part] = product
            else:
                out[0, 0, part] = (product * (1.0 / SPECTRA_SUMMED)).astype(out.dtype)


def on_device(voltages, fir_taps, channels, input_good_mask, tile_map):
    n_chan, n_tile = lax.axis_size("chan"), lax.axis_size("tile")
    side = 2 * n_chan * n_tile // (n_tile // 8 + 2)
    volts = voltages.reshape(2, FRAMES, GROUPS, LANES).transpose(1, 2, 0, 3)
    vmem = pl.BlockSpec(memory_space=pltpu.VMEM)
    smem = pl.BlockSpec(memory_space=pltpu.SMEM)
    hbm = pl.BlockSpec(memory_space=pltpu.HBM)
    dma = pltpu.SemaphoreType.DMA
    hops = (CHUNKS, 2, 2, n_tile // 4)
    return pl.pallas_call(
        lambda *refs: kernel(n_chan, n_tile, *refs),
        name="channelize_correlate",
        out_shape=jax.ShapeDtypeStruct((1, 1, 2, side, side), jnp.bfloat16),
        in_specs=[hbm, hbm, vmem, smem, smem],
        out_specs=vmem,
        scratch_shapes=[
            pltpu.VMEM((GROUPS, FRAMES + 1, 2, LANES), jnp.bfloat16),
            pltpu.VMEM((FILTER_TAPS, TRANSFORM_LENGTH), jnp.float32),
            pltpu.VMEM((2 * (CHUNK + FILTER_TAPS), LANES), jnp.float32),
            pltpu.VMEM((2 * CHUNK, TRANSFORM_LENGTH), jnp.bfloat16),
            pltpu.VMEM((2 * n_chan, TRANSFORM_LENGTH), jnp.bfloat16),
            pltpu.VMEM((2 * n_chan, LANES), jnp.float32),
            pltpu.VMEM((n_tile // 8 + 2, side, 2 * LANES), jnp.bfloat16),
            pltpu.VMEM((2, side, side), jnp.float32),
            *[pltpu.VMEM((2, n_chan, 2, LANES), jnp.bfloat16)] * CHUNKS,
            *[pltpu.VMEM((2, n_tile, n_chan, 2, LANES), jnp.bfloat16)] * CHUNKS,
            dma((GROUPS,)),
            dma,
            dma((CHUNKS,)),
            dma((CHUNKS,)),
            dma(hops),
            dma(hops),
            dma((CHUNKS,)),
            dma((CHUNKS,)),
        ],
        compiler_params=pltpu.CompilerParams(
            collective_id=0, has_side_effects=True, vmem_limit_bytes=60 * 1024 * 1024
        ),
    )(volts, fir_taps, channels.reshape(1, -1), input_good_mask, tile_map.T)


def solution(mesh):
    in_specs = (P("tile", "chan", None), P(), P(), P("tile", "chan"), P())
    out_specs = P("chan", "tile", None, None, None)
    return jax.shard_map(
        on_device, mesh=mesh, in_specs=in_specs, out_specs=out_specs, check_vma=False
    )
```

time: 179 us -> 63.9 us (0.36)
  the two profiles are of different devices: /device:TPU:2 before, /device:TPU:16 now
where the time goes in v2:
time: 63.9 us; the launch traced here: 63.6 us
  Pallas kernels  61.4 us (96%)
  local copies, waits for them, and re-layouts  2.26 us (4%)
    pallas_call x1, Pallas kernels, on_device(): pl.pallas_call(lambda *refs: kernel(n_chan, n_tile, *refs), name='channel...  61.4 us
    unnamed x1, local copies, waits for them, and re-layouts  2.26 us

profile of v2, /device:TPU:16, one launch (start us, length us, event | category | flops | bytes accessed | tf_op | source)
XLA Modules:
  0.0 63.6 jit_solution(14979784828347153705)
XLA Ops:
  0.0 61.4 %channelize_correlate.1 = bf16[1,1,2,512,512]{4,3,2,1,0:T(8,128)(2,1)} custom-call(bf16[271,16,2,128]{3,2,1,0:T(2,128)(2,1)} %bitcast.5, f32[16,2048]{1,0:T(8,128)} %refs_1_.1, s32[1,64]{1,0:T(1,128)} %bitcast.7, s32[1,2]{1,0:T(1,128)} %refs_3_.1, s32[16,64]{1,0:T(8,128)} %bitcast.6), custom_call_target="tpu_custom_call" | custom-call | tf_op jit(solution)/shard_map/channelize_correlate/pallas_call | solution.py:224
  61.4 2.3 %copy.7 = bf16[1,1,2,512,512]{4,3,2,1,0:T(8,128)(2,1)} copy(bf16[1,1,2,512,512]{4,3,2,1,0:T(8,128)(2,1)} %channelize_correlate.1) | data formatting | bytes 2097152

commit v3 on v2

--- a/solution.py
+++ b/solution.py
@@ -20,8 +20,8 @@
 BY_LANES = (((1,), (1,)), ((), ()))
 
 RING_ORDER = (
-    (0, 0, 1), (1, 0, 1), (0, 0, 2), (1, 0, 2), (0, 1, 1), (0, 0, 3), (1, 0, 3), (1, 1, 1),
-    (0, 1, 2), (0, 0, 4), (1, 0, 4), (1, 1, 2), (0, 1, 3), (1, 1, 3), (0, 1, 4), (1, 1, 4),
+    (0, 0, 1), (0, 0, 2), (0, 0, 3), (1, 0, 1), (0, 1, 1), (1, 0, 2), (0, 1, 2), (0, 0, 4),
+    (1, 1, 1), (0, 1, 3), (1, 1, 2), (1, 0, 3), (1, 1, 3), (0, 1, 4), (1, 0, 4), (1, 1, 4),
 )
 
 
@@ -216,6 +216,9 @@
     n_chan, n_tile = lax.axis_size("chan"), lax.axis_size("tile")
     side = 2 * n_chan * n_tile // (n_tile // 8 + 2)
     volts = voltages.reshape(2, FRAMES, GROUPS, LANES).transpose(1, 2, 0, 3)
+    volts, fir_taps = (
+        pltpu.with_memory_space_constraint(a, pltpu.HBM) for a in (volts, fir_taps)
+    )
     vmem = pl.BlockSpec(memory_space=pltpu.VMEM)
     smem = pl.BlockSpec(memory_space=pltpu.SMEM)
     hbm = pl.BlockSpec(memory_space=pltpu.HBM)
@@ -248,7 +251,7 @@
             dma((CHUNKS,)),
         ],
         compiler_params=pltpu.CompilerParams(
-            collective_id=0, has_side_effects=True, vmem_limit_bytes=60 * 1024 * 1024
+            collective_id=0, has_side_effects=True, vmem_limit_bytes=48 * 1024 * 1024
         ),
     )(volts, fir_taps, channels.reshape(1, -1), input_good_mask, tile_map.T)
 

time: 63.9 us -> 64.7 us (1.013)
  local copies, waits for them, and re-layouts: 2.26 us -> 2.98 us
    unnamed x1 -> x7, local copies, waits for them, and re-layouts: 2.26 us -> 2.98 us
where the time goes in v3:
time: 64.7 us; the launch traced here: 64.5 us
  Pallas kernels  61.5 us (95%)
  local copies, waits for them, and re-layouts  2.98 us (5%)
    pallas_call x1, Pallas kernels, on_device(): pl.pallas_call(lambda *refs: kernel(n_chan, n_tile, *refs), name='channel...  61.5 us
    unnamed x7, local copies, waits for them, and re-layouts  2.98 us

profile of v3, /device:TPU:16, one launch (start us, length us, event | category | flops | bytes accessed | tf_op | source)
XLA Modules:
  0.0 64.5 jit_solution(3997481912974774617)
XLA Ops:
  0.0 0.0 copy-start
  0.0 0.7 %copy-done = s32[64,16]{0,1:T(8,128)S(1)} copy-done((s32[64,16]{0,1:T(8,128)S(1)}, s32[64,16]{0,1:T(8,128)}, u32[]{:S(2)}) %copy-start) | copy-done | bytes 4120
  0.7 0.0 copy-start.1
  0.7 0.7 %copy-done.1 = s32[64]{0:T(128)S(1)} copy-done((s32[64]{0:T(128)S(1)}, s32[64]{0:T(128)}, u32[]{:S(2)}) %copy-start.1) | copy-done | bytes 280
  1.4 0.0 copy-start.2
  1.4 0.7 %copy-done.2 = s32[1,2]{1,0:T(1,128)S(1)} copy-done((s32[1,2]{1,0:T(1,128)S(1)}, s32[1,2]{1,0:T(1,128)}, u32[]{:S(2)}) %copy-start.2) | copy-done | bytes 32
  2.0 61.5 %channelize_correlate.1 = bf16[1,1,2,512,512]{4,3,2,1,0:T(8,128)(2,1)S(1)} custom-call(bf16[271,16,2,128]{3,2,1,0:T(2,128)(2,1)} %bitcast.7, f32[16,2048]{1,0:T(8,128)} %refs_1_.1, s32[1,64]{1,0:T(1,128)S(1)} %bitcast.6, s32[1,2]{1,0:T(1,128)S(1)} %copy-done.2, s32[16,64]{1,0:T(8,128)S(1)} %bitcast.5), custom_call_target="tpu_custom_call" | custom-call | tf_op jit(solution)/shard_map/channelize_correlate/pallas_call | solution.py:227
  63.5 1.0 %copy.7 = bf16[1,1,2,512,512]{4,3,2,1,0:T(8,128)(2,1)} copy(bf16[1,1,2,512,512]{4,3,2,1,0:T(8,128)(2,1)S(1)} %channelize_correlate.1) | data formatting | bytes 2097152
Async XLA Ops:
  0.0 0.7 %copy-start = (s32[64,16]{0,1:T(8,128)S(1)}, s32[64,16]{0,1:T(8,128)}, u32[]{:S(2)}) copy-start(s32[64,16]{0,1:T(8,128)} %param.9) | copy-start | bytes 12292
  0.7 0.7 %copy-start.1 = (s32[64]{0:T(128)S(1)}, s32[64]{0:T(128)}, u32[]{:S(2)}) copy-start(s32[64]{0:T(128)} %param.7) | copy-start | bytes 772
  1.4 0.7 %copy-start.2 = (s32[1,2]{1,0:T(1,128)S(1)}, s32[1,2]{1,0:T(1,128)}, u32[]{:S(2)}) copy-start(s32[1,2]{1,0:T(1,128)} %refs_3_.1) | copy-start | bytes 28

commit v4 on v3

--- a/solution.py
+++ b/solution.py
@@ -70,11 +70,11 @@
 
 
 def kernel(
-    n_chan, n_tile, volts, taps_hbm, channels, flags, tile_map, out,
-    slab, taps, wide, filtered, table, mixed, gathered, totals, *rest,
+    n_chan, n_tile, volts, taps_hbm, channels_hbm, flags_hbm, map_hbm, out,
+    slab, taps, channels, flags, tile_map, wide, filtered, table, mixed, totals, *rest,
 ):
     send, whole = rest[:CHUNKS], rest[CHUNKS : 2 * CHUNKS]
-    load_sem, taps_sem, turn_send, turn_recv, ring_send, ring_recv, pair_send, pair_recv = rest[
+    load_sem, small_sem, turn_send, turn_recv, ring_send, ring_recv, pair_send, pair_recv = rest[
         2 * CHUNKS :
     ]
     me = lax.axis_index("chan")
@@ -90,8 +90,14 @@
             volts.at[:, group], slab.at[group, pl.ds(0, FRAMES)], load_sem.at[group]
         )
 
-    load_taps = pltpu.make_async_copy(taps_hbm, taps, taps_sem)
-    load_taps.start()
+    small = [
+        pltpu.make_async_copy(source, target, small_sem.at[index])
+        for index, (source, target) in enumerate(
+            ((channels_hbm, channels), (taps_hbm, taps), (flags_hbm, flags), (map_hbm, tile_map))
+        )
+    ]
+    for copy in small:
+        copy.start()
     for group in range(GROUPS):
         load(group).start()
 
@@ -106,8 +112,10 @@
     for other in (ahead, behind, pair):
         pl.semaphore_signal(barrier, inc=1, device_id={"tile": other}, device_id_type=MESH)
 
+    small[0].wait()
     fill_table(channels[...], table)
-    load_taps.wait()
+    for copy in small[1:]:
+        copy.wait()
 
     for chunk in range(CHUNKS):
 
@@ -123,7 +131,7 @@
         )
         for part in (0, 1):
             for antenna in (0, 1):
-                flag = flags[0, antenna].astype(jnp.float32)
+                flag = flags[0:1, antenna : antenna + 1].astype(jnp.float32)
                 block = spectra[
                     part * n_chan : (part + 1) * n_chan, antenna * CHUNK : (antenna + 1) * CHUNK
                 ]
@@ -172,6 +180,28 @@
             device_id={"tile": ahead if direction == 0 else behind}, device_id_type=MESH,
         )
 
+    slot = tile_map[pl.ds(here, 1), :]
+    mine = lax.broadcasted_iota(jnp.int32, slot.shape, 1) == me
+
+    def weights(position):
+        made = []
+        for block in range(grid_side):
+            hit = jnp.where(mine, jnp.where(position == block, 1.0, 0.0), 0.0)
+            weight = jnp.sum(hit, axis=1, keepdims=True)
+            weight = jnp.broadcast_to(weight, (16, LANES)).astype(jnp.bfloat16)
+            made.append(jnp.concatenate([weight] * (side // 16), axis=0))
+        return made
+
+    row_weights = weights(lax.div(slot, grid_side))
+    col_weights = weights(lax.rem(slot, grid_side))
+
+    def chosen(flat, weight, part):
+        picked = None
+        for block in range(grid_side):
+            term = flat[pl.ds((part * grid_side + block) * side, side), :] * weight[block]
+            picked = term if picked is None else picked + term
+        return picked
+
     for chunk, column, step in RING_ORDER:
         if step == 1 and column == 0:
             turned(chunk).wait()
@@ -183,25 +213,16 @@
                 hop(chunk, direction, column, step - 1).wait_recv()
             hop(chunk, direction, column, step).start()
 
-    tile = tile_map[here, me]
     for chunk in range(CHUNKS):
         for column in (0, 1):
             for direction in (0, 1):
                 hop(chunk, direction, column, last).wait_recv()
-        across(chunk).wait_send()
-        for _, column, step in [entry for entry in RING_ORDER if entry[0] == chunk]:
-            for direction in (0, 1):
-                hop(chunk, direction, column, step).wait_send()
         inputs = 2 * n_chan * n_tile
         flat = whole[chunk].reshape(2 * inputs, LANES)
-        for part in (0, 1):
-            for block in range(grid_side):
-                gathered[block, :, part * LANES : (part + 1) * LANES] = flat[
-                    pl.ds(part * inputs + block * side, side), :
-                ]
-        rows = gathered[lax.div(tile, grid_side)]
-        straight = gathered[lax.rem(tile, grid_side)]
-        crossed = jnp.concatenate([straight[:, LANES:], -straight[:, :LANES]], axis=1)
+        rows = jnp.concatenate([chosen(flat, row_weights, part) for part in (0, 1)], axis=1)
+        col_real, col_imag = [chosen(flat, col_weights, part) for part in (0, 1)]
+        straight = jnp.concatenate([col_real, col_imag], axis=1)
+        crossed = jnp.concatenate([col_imag, -col_real], axis=1)
         for part, cols in enumerate((straight, crossed)):
             product = lax.dot_general(rows, cols, BY_LANES, preferred_element_type=jnp.float32)
             if chunk > 0:
@@ -210,17 +231,20 @@
                 totals[part] = product
             else:
                 out[0, 0, part] = (product * (1.0 / SPECTRA_SUMMED)).astype(out.dtype)
+    for chunk in range(CHUNKS):
+        across(chunk).wait_send()
+    for chunk, column, step in RING_ORDER:
+        for direction in (0, 1):
+            hop(chunk, direction, column, step).wait_send()
 
 
 def on_device(voltages, fir_taps, channels, input_good_mask, tile_map):
     n_chan, n_tile = lax.axis_size("chan"), lax.axis_size("tile")
     side = 2 * n_chan * n_tile // (n_tile // 8 + 2)
     volts = voltages.reshape(2, FRAMES, GROUPS, LANES).transpose(1, 2, 0, 3)
-    volts, fir_taps = (
-        pltpu.with_memory_space_constraint(a, pltpu.HBM) for a in (volts, fir_taps)
-    )
+    operands = (volts, fir_taps, channels.reshape(1, -1), input_good_mask, tile_map.T)
+    operands = [pltpu.with_memory_space_constraint(a, pltpu.HBM) for a in operands]
     vmem = pl.BlockSpec(memory_space=pltpu.VMEM)
-    smem = pl.BlockSpec(memory_space=pltpu.SMEM)
     hbm = pl.BlockSpec(memory_space=pltpu.HBM)
     dma = pltpu.SemaphoreType.DMA
     hops = (CHUNKS, 2, 2, n_tile // 4)
@@ -228,21 +252,20 @@
         lambda *refs: kernel(n_chan, n_tile, *refs),
         name="channelize_correlate",
         out_shape=jax.ShapeDtypeStruct((1, 1, 2, side, side), jnp.bfloat16),
-        in_specs=[hbm, hbm, vmem, smem, smem],
+        in_specs=[hbm] * len(operands),
         out_specs=vmem,
         scratch_shapes=[
             pltpu.VMEM((GROUPS, FRAMES + 1, 2, LANES), jnp.bfloat16),
-            pltpu.VMEM((FILTER_TAPS, TRANSFORM_LENGTH), jnp.float32),
+            *[pltpu.VMEM(a.shape, a.dtype) for a in operands[1:]],
             pltpu.VMEM((2 * (CHUNK + FILTER_TAPS), LANES), jnp.float32),
             pltpu.VMEM((2 * CHUNK, TRANSFORM_LENGTH), jnp.bfloat16),
             pltpu.VMEM((2 * n_chan, TRANSFORM_LENGTH), jnp.bfloat16),
             pltpu.VMEM((2 * n_chan, LANES), jnp.float32),
-            pltpu.VMEM((n_tile // 8 + 2, side, 2 * LANES), jnp.bfloat16),
             pltpu.VMEM((2, side, side), jnp.float32),
             *[pltpu.VMEM((2, n_chan, 2, LANES), jnp.bfloat16)] * CHUNKS,
             *[pltpu.VMEM((2, n_tile, n_chan, 2, LANES), jnp.bfloat16)] * CHUNKS,
             dma((GROUPS,)),
-            dma,
+            dma((4,)),
             dma((CHUNKS,)),
             dma((CHUNKS,)),
             dma(hops),
@@ -253,7 +276,7 @@
         compiler_params=pltpu.CompilerParams(
             collective_id=0, has_side_effects=True, vmem_limit_bytes=48 * 1024 * 1024
         ),
-    )(volts, fir_taps, channels.reshape(1, -1), input_good_mask, tile_map.T)
+    )(*operands)
 
 
 def solution(mesh):

time: 64.7 us -> 62.9 us (0.972)
  local copies, waits for them, and re-layouts: 2.98 us -> 0.97 us
    unnamed x7 -> x1, local copies, waits for them, and re-layouts: 2.98 us -> 0.97 us
where the time goes in v4:
time: 62.9 us; the launch traced here: 62.7 us
  Pallas kernels  61.7 us (98%)
  local copies, waits for them, and re-layouts  0.97 us (2%)
    pallas_call x1, Pallas kernels, on_device(): pl.pallas_call(lambda *refs: kernel(n_chan, n_tile, *refs), name='channel...  61.7 us

profile of v4, /device:TPU:16, one launch (start us, length us, event | category | flops | bytes accessed | tf_op | source)
XLA Modules:
  0.0 62.7 jit_solution(4399292578922324556)
XLA Ops:
  0.0 61.7 %channelize_correlate.1 = bf16[1,1,2,512,512]{4,3,2,1,0:T(8,128)(2,1)S(1)} custom-call(bf16[271,16,2,128]{3,2,1,0:T(2,128)(2,1)} %bitcast.5, f32[16,2048]{1,0:T(8,128)} %refs_1_.1, s32[1,64]{1,0:T(1,128)} %bitcast.7, s32[1,2]{1,0:T(1,128)} %refs_3_.1, s32[16,64]{1,0:T(8,128)} %bitcast.6), custom_call_target="tpu_custom_call" | custom-call | tf_op jit(solution)/shard_map/channelize_correlate/pallas_call | solution.py:251
  61.7 1.0 %copy.7 = bf16[1,1,2,512,512]{4,3,2,1,0:T(8,128)(2,1)} copy(bf16[1,1,2,512,512]{4,3,2,1,0:T(8,128)(2,1)S(1)} %channelize_correlate.1) | data formatting | bytes 2097152

commit v5 on v4

--- a/solution.py
+++ b/solution.py
@@ -204,7 +204,7 @@
 
     for chunk, column, step in RING_ORDER:
         if step == 1 and column == 0:
-            turned(chunk).wait()
+            turned(chunk).wait_recv()
             across(chunk).start()
         if step == 1 and column == 1:
             across(chunk).wait_recv()
@@ -232,6 +232,7 @@
             else:
                 out[0, 0, part] = (product * (1.0 / SPECTRA_SUMMED)).astype(out.dtype)
     for chunk in range(CHUNKS):
+        turned(chunk).wait_send()
         across(chunk).wait_send()
     for chunk, column, step in RING_ORDER:
         for direction in (0, 1):

time: 62.9 us -> 62.9 us (level)
  no operation moved by 1% of the time
where the time goes in v5:
time: 62.9 us; the launch traced here: 62.7 us
  Pallas kernels  61.7 us (98%)
  local copies, waits for them, and re-layouts  0.97 us (2%)
    pallas_call x1, Pallas kernels, on_device(): pl.pallas_call(lambda *refs: kernel(n_chan, n_tile, *refs), name='channel...  61.7 us

profile of v5, /device:TPU:16, one launch (start us, length us, event | category | flops | bytes accessed | tf_op | source)
XLA Modules:
  0.0 62.7 jit_solution(1290262160955888254)
XLA Ops:
  0.0 61.7 %channelize_correlate.1 = bf16[1,1,2,512,512]{4,3,2,1,0:T(8,128)(2,1)S(1)} custom-call(bf16[271,16,2,128]{3,2,1,0:T(2,128)(2,1)} %bitcast.5, f32[16,2048]{1,0:T(8,128)} %refs_1_.1, s32[1,64]{1,0:T(1,128)} %bitcast.7, s32[1,2]{1,0:T(1,128)} %refs_3_.1, s32[16,64]{1,0:T(8,128)} %bitcast.6), custom_call_target="tpu_custom_call" | custom-call | tf_op jit(solution)/shard_map/channelize_correlate/pallas_call | solution.py:252
  61.7 1.0 %copy.7 = bf16[1,1,2,512,512]{4,3,2,1,0:T(8,128)(2,1)} copy(bf16[1,1,2,512,512]{4,3,2,1,0:T(8,128)(2,1)S(1)} %channelize_correlate.1) | data formatting | bytes 2097152
